TPU v7x, 32 devices: a whole 2x2x4 slice. The times are simulated.
32 devices in a mesh: prompt: 4 (over z), tensor: 8 (over y, x, core).
Axes of the slice: x: 2, y: 2, z: 4, core: 2. Of those that a mesh axis runs over, the one named last changes fastest.
Arguments:
- embeds: bfloat16 [4, 64, 8192], P('prompt', None, 'tensor'), may hold values from -400 to 400
- norm_gain: bfloat16 [8192], replicated, may hold values from 0.5 to 1.5
- query_weight: bfloat16 [8192, 8192], P('prompt', 'tensor'), may hold values from -1 to 1
- key_weight: bfloat16 [8192, 1024], P('prompt', 'tensor'), may hold values from -6 to 6
- value_weight: bfloat16 [8192, 1024], P('prompt', 'tensor'), may hold values from -0.0625 to 0.0625
- out_weight: bfloat16 [8192, 8192], P('tensor', 'prompt'), may hold values from -0.0625 to 0.0625
- out_grad: bfloat16 [4, 64, 8192], P('prompt', None, 'tensor'), may hold values from -6 to 6
- suffix_pos: int32 [4, 20], P('prompt'), may hold values from 0 to 63
- vocab_table: bfloat16 [65536, 8192], P(('prompt', 'tensor')), may hold values from -0.0625 to 0.0625
- banned: int32 [65536], P(('prompt', 'tensor')), may hold values 0 or 1
Outputs:
- token_scores: float32 [4, 20, 65536], P(None, None, ('prompt', 'tensor'))
All inputs are finite; a program needn't handle non-finite values. No bound on the sum of `banned` on one device may be relied on, other than what follows from the above.
Results may differ from a plain program's by a relative error of at most 0.01.
The roundings to bfloat16 on the way count: a program that leaves them out, or rounds other values in their place, can miss the bound.
Values may be sent and summed in bfloat16 or wider, within the bound.
A program may use at most 192 MiB of HBM per device.

v0:
```python
import math
import jax
import jax.numpy as jnp
from jax import lax
from jax.sharding import PartitionSpec as P

KVH = 8
HD = 128
EPSILON = 1e-05


def dot_f32(spec, a, b):
    return jnp.einsum(spec, a, b, preferred_element_type=jnp.float32)


def on_device(
    embeds,
    norm_gain,
    query_weight,
    key_weight,
    value_weight,
    out_weight,
    out_grad,
    suffix_pos,
    vocab_table,
    banned,
):
    n_prompt = lax.axis_size("prompt")
    n_tensor = lax.axis_size("tensor")
    here_prompt = lax.axis_index("prompt")
    here_tensor = lax.axis_index("tensor")
    seq_len = embeds.shape[1]
    suffix_count = suffix_pos.shape[1]
    width = embeds.shape[2] * n_tensor
    rows_here, head_cols = query_weight.shape
    key_cols = key_weight.shape[1]
    heads_here = head_cols // HD
    slice_width = rows_here // n_tensor
    logit_scale = 1.0 / math.sqrt(HD)
    suffix_all = lax.all_gather(suffix_pos, "prompt", axis=0, tiled=True)
    both = jnp.concatenate([embeds, out_grad], axis=1)
    both = lax.all_gather(both, "tensor", axis=2, tiled=True)
    own = both[:, :seq_len].astype(jnp.float32)
    inverse_norm = lax.rsqrt(jnp.mean(own * own, axis=-1, keepdims=True) + EPSILON)
    inverse_norm = lax.all_gather(inverse_norm, "prompt", axis=0, tiled=True)
    both = lax.all_to_all(both, "prompt", split_axis=2, concat_axis=0, tiled=True)
    embeds = both[:, :seq_len]
    out_grad = both[:, seq_len:]
    embeds_float = embeds.astype(jnp.float32)
    gain_rows = lax.dynamic_slice_in_dim(norm_gain, here_prompt * rows_here, rows_here, 0)
    gain_rows = gain_rows.astype(jnp.float32)
    normed = (embeds_float * inverse_norm * gain_rows).astype(jnp.bfloat16)
    parts = jnp.concatenate(
        [
            dot_f32("psd,dc->psc", normed, query_weight),
            dot_f32("psd,dc->psc", normed, key_weight),
            dot_f32("psd,dc->psc", normed, value_weight),
            dot_f32("psd,cd->psc", out_grad, out_weight),
        ],
        axis=2,
    )
    whole = lax.psum_scatter(parts, "prompt", scatter_dimension=0, tiled=True)
    whole = whole[0].astype(jnp.bfloat16)
    queries = whole[:, :head_cols].reshape(seq_len, heads_here, HD)
    key_values = whole[:, head_cols : head_cols + 2 * key_cols]
    contexts = whole[:, head_cols + 2 * key_cols :].reshape(seq_len, heads_here, HD)
    key_values = lax.all_gather(key_values, "tensor", axis=0, tiled=False)
    key_values = key_values.reshape(n_tensor, seq_len, 2, key_cols).transpose(2, 1, 0, 3)
    key_values = key_values.reshape(2, seq_len, KVH * HD)
    fold = min(heads_here, KVH)
    first = here_tensor * heads_here % KVH * HD
    if fold < KVH:
        key_values = lax.dynamic_slice_in_dim(key_values, first, fold * HD, 2)
    key_values = key_values.reshape(2, seq_len, fold, HD)
    if heads_here > fold:
        key_values = jnp.tile(key_values, (1, 1, heads_here // fold, 1))
    keys, values = (key_values[0], key_values[1])
    logits = dot_f32("qhd,khd->hqk", queries, keys) * logit_scale
    row_index = lax.broadcasted_iota(jnp.int32, (seq_len, seq_len), 0)
    col_index = lax.broadcasted_iota(jnp.int32, (seq_len, seq_len), 1)
    causal = col_index <= row_index
    largest = jnp.max(jnp.where(causal, logits, -1e30), axis=-1, keepdims=True)
    raised = jnp.where(causal, jnp.exp(logits - largest), 0.0)
    probs = raised / jnp.sum(raised, axis=-1, keepdims=True)
    probs_low = probs.astype(jnp.bfloat16)
    prob_grad = dot_f32("qhd,khd->hqk", contexts, values)
    logit_grad = (
        probs * (prob_grad - jnp.sum(prob_grad * probs, axis=-1, keepdims=True)) * logit_scale
    ).astype(jnp.bfloat16)
    steps_iota = lax.broadcasted_iota(jnp.int32, (suffix_count, seq_len), 1)
    chooser = (steps_iota == suffix_pos[0][:, None]).astype(jnp.bfloat16)
    logit_rows = dot_f32("ns,hsk->hnk", chooser, logit_grad).astype(jnp.bfloat16)
    query_grad = dot_f32("hnk,khd->nhd", logit_rows, keys).astype(jnp.bfloat16)
    query_grad = query_grad.reshape(suffix_count, head_cols)
    logit_cols = dot_f32("hqk,nk->hnq", logit_grad, chooser).astype(jnp.bfloat16)
    prob_cols = dot_f32("hqk,nk->hnq", probs_low, chooser).astype(jnp.bfloat16)
    key_each = dot_f32("hnq,qhd->nhd", logit_cols, queries)
    value_each = dot_f32("hnq,qhd->nhd", prob_cols, contexts)
    slots = jnp.stack([key_each, value_each])
    slots = slots.reshape(2, suffix_count, heads_here // fold, fold * HD).sum(axis=2)
    if fold < KVH:
        slots = lax.dynamic_update_slice_in_dim(
            jnp.zeros((2, suffix_count, KVH * HD), jnp.float32), slots, first, 2
        )
    grads = lax.psum_scatter(slots, "tensor", scatter_dimension=2, tiled=True)
    grads = grads.astype(jnp.bfloat16)
    grads = jnp.concatenate([query_grad, grads[0], grads[1]], axis=1)
    grads = lax.all_gather(grads, "prompt", axis=0, tiled=True)
    branch = dot_f32("nc,dc->nd", grads[:, :head_cols], query_weight)
    branch = branch + dot_f32("nc,dc->nd", grads[:, head_cols : head_cols + key_cols], key_weight)
    branch = branch + dot_f32("nc,dc->nd", grads[:, head_cols + key_cols :], value_weight)
    share = lax.psum_scatter(branch, "tensor", scatter_dimension=1, tiled=True)
    start = here_tensor * slice_width
    embeds_slice = lax.dynamic_slice_in_dim(embeds, start, slice_width, 2)
    steps_iota = lax.broadcasted_iota(jnp.int32, (n_prompt, suffix_count, seq_len), 2)
    chooser_all = steps_iota == suffix_all[:, :, None]
    embed_rows = dot_f32("pns,psd->pnd", chooser_all.astype(jnp.bfloat16), embeds_slice)
    norm_rows = jnp.sum(
        jnp.where(chooser_all, inverse_norm[:, None, :, 0], 0.0), axis=-1, keepdims=True
    )
    scaled = (embed_rows * norm_rows).reshape(n_prompt * suffix_count, slice_width)
    norm_rows = norm_rows.reshape(n_prompt * suffix_count, 1)
    gain_slice = lax.dynamic_slice_in_dim(gain_rows, start, slice_width, 0)
    weighted = share * gain_slice
    inner = jnp.sum(weighted * scaled, axis=-1, keepdims=True)
    inner = lax.psum(inner, ("prompt", "tensor")) / width
    suffix_grad = (norm_rows * (weighted - scaled * inner)).astype(jnp.bfloat16)
    flat_grads = lax.all_gather(suffix_grad, ("prompt", "tensor"), axis=1, tiled=True)
    scores = -dot_f32("rd,vd->rv", flat_grads, vocab_table)
    scores = scores.reshape(n_prompt, suffix_count, vocab_table.shape[0])
    return jnp.where(banned[None, None, :] == 1, 0.0, scores)


def solution(mesh):
    return jax.shard_map(
        on_device,
        mesh=mesh,
        in_specs=(
            P("prompt", None, "tensor"),
            P(),
            P("prompt", "tensor"),
            P("prompt", "tensor"),
            P("prompt", "tensor"),
            P("tensor", "prompt"),
            P("prompt", None, "tensor"),
            P("prompt", None),
            P(("prompt", "tensor"), None),
            P(("prompt", "tensor")),
        ),
        out_specs=P(None, None, ("prompt", "tensor")),
        check_vma=False,
    )
```

profile of v0, /device:TPU:0, one launch (start us, length us, event | category | flops | bytes accessed | tf_op | source)
XLA Modules:
  0.0 440.1 jit_solution(10545317299658269144)
XLA Ops:
  6.5 1.7 pad_maximum_fusion.1
  8.3 31.6 %all-gather.7.cloned.1.call-done = bf16[1,128,8192]{2,1,0:T(8,128)(2,1)} async-done(((bf16[1,128,1024]{2,1,0:T(8,128)(2,1)}), bf16[1,128,8192]{2,1,0:T(8,128)(2,1)}) %all-gather.7.cloned.1.call-update) | async-done | bytes 2097168 | tf_op jit(solution)/shard_map/all_gather | solution.py:42
  39.9 9.5 %copy.48 = bf16[1,128,8192]{1,0,2:T(2,128)(2,1)} copy(bf16[1,128,8192]{2,1,0:T(8,128)(2,1)} %all-gather.7.cloned.1.call-done) | data formatting | bytes 4194304 | tf_op jit(solution)/shard_map/all_gather | solution.py:42
  49.4 0.5 broadcast.47
  49.9 45.2 %reduce.1 = bf16[8192,128]{1,0:T(8,128)(2,1)S(1)} reduce(bf16[8192,1,128]{2,1,0:T(2,128)(2,1)} %bitcast.91, bf16[]{:T(256)} %broadcast.47), dimensions={1}, to_apply=%bitcast.83.reduce_sub_computation | reduce | bytes 4194306
  95.1 2.1 reshape.85
  97.2 4.7 %all-to-all-start = ((bf16[4,2,131072]{2,1,0:T(2,128)(2,1)}), bf16[4,2,131072]{2,1,0:T(2,128)(2,1)S(1)}, u32[]{:S(2)}, u32[]{:S(2)}) async-start(bf16[4,2,131072]{2,1,0:T(2,128)(2,1)} %reshape.85), calls=%async_computation | async-start | bytes 4194304 | tf_op jit(solution)/shard_map/all_to_all | solution.py:46
  101.9 0.6 dynamic-slice
  103.2 0.7 dynamic-slice_convert_fusion
  103.9 1.5 multiply_reduce_fusion
  105.5 36.9 %all-reduce = f32[256]{0:T(256)S(1)} all-reduce(f32[256]{0:T(256)S(1)} %rsqrt_dynamic-update-slice_fusion), channel_id=2, replica_groups=mesh['prompt'=4,'tensor'=8] {'prompt'}, use_global_device_ids=true, to_apply=%add | all-reduce | flops 256 | bytes 2048
  142.5 8.3 %all-to-all-done = bf16[4,2,131072]{2,1,0:T(2,128)(2,1)S(1)} async-done(((bf16[4,2,131072]{2,1,0:T(2,128)(2,1)}), bf16[4,2,131072]{2,1,0:T(2,128)(2,1)S(1)}, u32[]{:S(2)}, u32[]{:S(2)}) %all-to-all-start) | async-done | bytes 2097184 | tf_op jit(solution)/shard_map/all_to_all | solution.py:46
  150.8 3.4 reshape.86
  154.1 2.5 copy.67
  156.6 2.7 copy.49
  159.3 1.9 fusion.18
  161.3 0.5 fusion.19
  161.8 3.6 fusion.4
  165.4 1.3 fusion.2
  166.7 1.6 pad_maximum_fusion
  168.4 48.5 %reduce-scatter.4.cloned.1.call-done = f32[1,64,2304]{2,1,0:T(8,128)} async-done(((f32[4,64,2304]{2,1,0:T(8,128)}), f32[1,64,2304]{2,1,0:T(8,128)}) %reduce-scatter.4.cloned.1.call-update) | async-done | bytes 589840 | tf_op jit(solution)/shard_map/reduce_scatter | solution.py:62
  217.0 1.1 convert_bitcast_fusion
  218.1 9.5 %all-gather.1 = bf16[512,256]{1,0:T(8,128)(2,1)S(1)} all-gather(bf16[64,256]{1,0:T(8,128)(2,1)S(1)} %slice.55), channel_id=3, replica_groups=mesh['prompt'=4,'tensor'=8] {'tensor'}, dimensions={0}, use_global_device_ids=true | all-gather | bytes 294912 | tf_op jit(solution)/shard_map/all_gather | solution.py:67
  227.7 0.2 fusion.31
  227.9 0.2 convolution_multiply_fusion
  228.1 0.7 copy-done.4
  228.8 0.8 fusion.85
  229.6 1.4 convolution_bitcast_fusion
  231.0 1.4 convolution_bitcast_fusion.1
  232.4 0.7 maximum_bitcast_fusion
  233.2 1.7 fusion.14
  235.0 29.7 %reduce-scatter.6.cloned.1.call-done = f32[2,20,128]{2,1,0:T(8,128)} async-done(((f32[2,20,1024]{2,1,0:T(8,128)}), f32[2,20,128]{2,1,0:T(8,128)}) %reduce-scatter.6.cloned.1.call-update) | async-done | bytes 20496 | tf_op jit(solution)/shard_map/reduce_scatter | solution.py:105
  264.6 0.7 convert_element_type.69
  265.4 13.9 %all-gather.3 = bf16[4,20,1280]{2,1,0:T(8,128)(2,1)S(1)} all-gather(bf16[1,20,1280]{2,1,0:T(8,128)(2,1)S(1)} %maximum_bitcast_fusion.1), channel_id=1, replica_groups=mesh['prompt'=4,'tensor'=8] {'prompt'}, dimensions={0}, use_global_device_ids=true | all-gather | bytes 256000 | tf_op jit(solution)/shard_map/all_gather | solution.py:108
  279.3 0.3 fusion.49
  279.6 1.3 fusion.51
  280.9 4.4 %fusion.6 = f32[80,2048]{1,0:T(8,128)} fusion(f32[80,2048]{1,0:T(8,128)S(1)} %fusion.49, f32[80,2048]{1,0:T(8,128)S(1)} %fusion.51, bf16[2048,1024]{1,0:T(8,128)(2,1)} %param.12, bf16[80,1280]{1,0:T(8,128)(2,1)S(1)} %reshape.77), kind=kOutput, calls=%fused_computation.7 | convolution fusion | flops 335872000 | bytes 6324224 | tf_op jit(solution)/shard_map/nc,dc->nd/dot_general | solution.py:13
  285.6 11.1 %all-gather.2 = s32[4,1,20]{2,1,0:T(1,128)S(1)} all-gather(s32[1,1,20]{2,1,0:T(1,128)S(1)} %bitcast.112), channel_id=1, replica_groups=mesh['prompt'=4,'tensor'=8] {'prompt'}, dimensions={0}, use_global_device_ids=true | all-gather | bytes 400 | tf_op jit(solution)/shard_map/all_gather | solution.py:40
  296.7 0.2 select_reduce_fusion.1
  296.9 0.1 slice.53
  297.0 0.2 convolution_multiply_fusion.1
  297.2 23.2 %reduce-scatter.8.cloned.1.call-done = f32[80,256]{1,0:T(8,128)} async-done(((f32[80,2048]{1,0:T(8,128)}), f32[80,256]{1,0:T(8,128)}) %reduce-scatter.8.cloned.1.call-update) | async-done | bytes 81936 | tf_op jit(solution)/shard_map/reduce_scatter | solution.py:112
  320.5 1.0 multiply_reduce_fusion.2
  321.5 39.4 %psum.7 = f32[80,1]{0,1:T(1,128)S(1)} all-reduce(f32[80,1]{0,1:T(1,128)S(1)} %bitcast.108), channel_id=1, replica_groups=mesh['prompt'=4,'tensor'=8] {'prompt','tensor'}, use_global_device_ids=true, to_apply=%region_9.10 | all-reduce | flops 80 | bytes 640 | tf_op jit(solution)/shard_map/psum | solution.py:126
  360.9 1.6 multiply_convert_fusion.4
  362.5 54.4 %all-gather.9.cloned.1.call-done = bf16[80,8192]{1,0:T(8,128)(2,1)} async-done(((bf16[80,256]{1,0:T(8,128)(2,1)}), bf16[80,8192]{1,0:T(8,128)(2,1)}) %all-gather.9.cloned.1.call-update) | async-done | bytes 1310736 | tf_op jit(solution)/shard_map/all_gather | solution.py:128
  416.9 15.3 %convolution_negate_fusion = f32[80,2048]{1,0:T(8,128)S(1)} fusion(bf16[80,8192]{1,0:T(8,128)(2,1)} %all-gather.9.cloned.1.call-done, bf16[2048,8192]{1,0:T(8,128)(2,1)} %param.18), kind=kOutput, calls=%fused_computation.8 | convolution fusion | flops 2684518400 | bytes 35520512 | tf_op jit(solution)/shard_map/rd,vd->rv/dot_general | solution.py:13
  432.4 1.3 copy.63
  (52 shorter events, 1.2 us)
Async XLA Ops:
  6.5 152.8 %copy-start = (bf16[2048,128]{1,0:T(8,128)(2,1)S(1)}, bf16[2048,128]{1,0:T(8,128)(2,1)}, u32[]{:S(2)}) copy-start(bf16[2048,128]{1,0:T(8,128)(2,1)} %param.14) | copy-start | bytes 1572868
  6.5 33.4 %all-gather.7.cloned.1.call-start = ((), (), s32[]{:S(2)}) async-start(), calls=%async_computation.4 | async-start | bytes 2359296 | tf_op jit(solution)/shard_map/all_gather | solution.py:42
  97.2 4.7 %copy-start.8 = (u32[32]{0:T(128)S(1)}, u32[32]{0:T(128)}, u32[]{:S(2)}) copy-start(u32[32]{0:T(128)} %constant.38) | copy-start | bytes 388
  97.2 53.6 %all-to-all-start = ((bf16[4,2,131072]{2,1,0:T(2,128)(2,1)}), bf16[4,2,131072]{2,1,0:T(2,128)(2,1)S(1)}, u32[]{:S(2)}, u32[]{:S(2)}) async-start(bf16[4,2,131072]{2,1,0:T(2,128)(2,1)} %reshape.85), calls=%async_computation | async-start | bytes 4194304 | tf_op jit(solution)/shard_map/all_to_all | solution.py:46
  101.9 115.0 %reduce-scatter.4.cloned.1.call-start = ((), (), s32[]{:S(2)}) async-start(), calls=%async_computation.5 | async-start | bytes 2949120 | tf_op jit(solution)/shard_map/reduce_scatter | solution.py:62
  159.3 1.9 copy-start.1
  159.3 2.0 copy-start.2
  161.8 3.7 copy-start.7
  168.4 96.2 %reduce-scatter.6.cloned.1.call-start = ((), (), s32[]{:S(2)}) async-start(), calls=%async_computation.6 | async-start | bytes 221184 | tf_op jit(solution)/shard_map/reduce_scatter | solution.py:105
  168.4 61.2 %copy-start.6 = (s32[1,20]{1,0:T(1,128)S(1)}, s32[1,20]{1,0:T(1,128)}, u32[]{:S(2)}) copy-start(s32[1,20]{1,0:T(1,128)} %param.17) | copy-start | bytes 244
  227.9 3.1 copy-start.3
  228.1 0.7 copy-start.4
  233.2 87.3 %reduce-scatter.8.cloned.1.call-start = ((), (), s32[]{:S(2)}) async-start(), calls=%async_computation.7 | async-start | bytes 737280 | tf_op jit(solution)/shard_map/reduce_scatter | solution.py:112
  285.4 77.1 %copy-start.5 = (s32[2048]{0:T(1024)S(1)}, s32[2048]{0:T(1024)}, u32[]{:S(2)}) copy-start(s32[2048]{0:T(1024)} %param.19) | copy-start | bytes 24580
  285.4 131.5 %all-gather.9.cloned.1.call-start = ((), (), s32[]{:S(2)}) async-start(), calls=%async_computation.8 | async-start | bytes 1351680 | tf_op jit(solution)/shard_map/all_gather | solution.py:128
Sparse Core Ops, SparseCore 0:
  9.3 30.5 all-gather.6
  168.5 48.4 reduce-scatter.3
  233.3 31.2 reduce-scatter.5
  285.5 34.8 reduce-scatter.7
  362.6 54.2 all-gather.8
where the time goes:
time: 441 us; the launch traced here: 440 us
  waiting for transfers between devices  196 us (44%)
  blocking collectives  111 us (25%)
  other arithmetic  57 us (13%)
  matrix products  33.6 us (8%)
  local copies, waits for them, and re-layouts  24 us (5%)
  between operations  14.1 us (3%)
  starting transfers between devices  4.86 us (1%)
    all_gather x1, waiting for transfers between devices, on_device(): lax.all_gather(suffix_grad, ('prompt', 'tensor'), axis=1, tiled=True)  54.4 us
    reduce_scatter x1, waiting for transfers between devices, on_device(): whole = lax.psum_scatter(parts, 'prompt', scatter_dimension=0, tiled=True)  48.5 us
    unnamed x3, other arithmetic  45.3 us
    psum x1, blocking collectives, on_device(): inner = lax.psum(inner, ('prompt', 'tensor')) / width  39.4 us
    unnamed x1, blocking collectives  36.9 us
    dot_general x14, matrix products, dot_f32(): return jnp.einsum(spec, a, b, preferred_element_type=jnp.float32)  33.6 us
    all_gather x1, waiting for transfers between devices, on_device(): both = lax.all_gather(both, 'tensor', axis=2, tiled=True)  31.6 us
    reduce_scatter x1, waiting for transfers between devices, on_device(): grads = lax.psum_scatter(slots, 'tensor', scatter_dimension=2, tiled=True)  29.7 us
  transfers between devices with their start and end apart: 6, of which 6 were waited for; matrix products, arithmetic and copies ran while one was open for 1% of the time, Pallas kernels for 0%

commit v1 on v0

--- a/solution.py
+++ b/solution.py
@@ -7,6 +7,11 @@
 KVH = 8
 HD = 128
 EPSILON = 1e-05
+
+
+def by_each_axis(array, inner_axis, outer_axis):
+    half = lax.psum(array, inner_axis)
+    return lax.psum(half, outer_axis)
 
 
 def dot_f32(spec, a, b):
@@ -123,7 +128,7 @@
     gain_slice = lax.dynamic_slice_in_dim(gain_rows, start, slice_width, 0)
     weighted = share * gain_slice
     inner = jnp.sum(weighted * scaled, axis=-1, keepdims=True)
-    inner = lax.psum(inner, ("prompt", "tensor")) / width
+    inner = by_each_axis(inner, "tensor", "prompt") / width
     suffix_grad = (norm_rows * (weighted - scaled * inner)).astype(jnp.bfloat16)
     flat_grads = lax.all_gather(suffix_grad, ("prompt", "tensor"), axis=1, tiled=True)
     scores = -dot_f32("rd,vd->rv", flat_grads, vocab_table)

time: 441 us -> 423 us (0.959)
  blocking collectives: 111 us -> 95.3 us
    psum x1 -> x2, blocking collectives: 39.4 us -> 24 us  [the longest x1 12.3 us: by_each_axis(): half = lax.psum(array, inner_axis)]
where the time goes in v1:
time: 423 us; the launch traced here: 421 us
  waiting for transfers between devices  192 us (45%)
  blocking collectives  95.3 us (23%)
  other arithmetic  57 us (13%)
  matrix products  33.6 us (8%)
  local copies, waits for them, and re-layouts  24 us (6%)
  between operations  14.1 us (3%)
  starting transfers between devices  4.86 us (1%)
    all_gather x1, waiting for transfers between devices, on_device(): lax.all_gather(suffix_grad, ('prompt', 'tensor'), axis=1, tiled=True)  51.1 us
    reduce_scatter x1, waiting for transfers between devices, on_device(): whole = lax.psum_scatter(parts, 'prompt', scatter_dimension=0, tiled=True)  48.5 us
    unnamed x3, other arithmetic  45.3 us
    unnamed x1, blocking collectives  36.9 us
    dot_general x14, matrix products, dot_f32(): return jnp.einsum(spec, a, b, preferred_element_type=jnp.float32)  33.6 us
    all_gather x1, waiting for transfers between devices, on_device(): both = lax.all_gather(both, 'tensor', axis=2, tiled=True)  31.6 us
    reduce_scatter x1, waiting for transfers between devices, on_device(): grads = lax.psum_scatter(slots, 'tensor', scatter_dimension=2, tiled=True)  29.7 us
    reduce_scatter x1, waiting for transfers between devices, on_device(): share = lax.psum_scatter(branch, 'tensor', scatter_dimension=1, tiled=True)  23.2 us
  transfers between devices with their start and end apart: 6, of which 6 were waited for; matrix products, arithmetic and copies ran while one was open for 1% of the time, Pallas kernels for 0%

profile of v1, /device:TPU:0, one launch (start us, length us, event | category | flops | bytes accessed | tf_op | source)
XLA Modules:
  0.0 421.4 jit_solution(12735539787260669906)
XLA Ops:
  6.5 1.7 pad_maximum_fusion.1
  8.3 31.6 %all-gather.7.cloned.1.call-done = bf16[1,128,8192]{2,1,0:T(8,128)(2,1)} async-done(((bf16[1,128,1024]{2,1,0:T(8,128)(2,1)}), bf16[1,128,8192]{2,1,0:T(8,128)(2,1)}) %all-gather.7.cloned.1.call-update) | async-done | bytes 2097168 | tf_op jit(solution)/shard_map/all_gather | solution.py:47
  39.9 9.5 %copy.48 = bf16[1,128,8192]{1,0,2:T(2,128)(2,1)} copy(bf16[1,128,8192]{2,1,0:T(8,128)(2,1)} %all-gather.7.cloned.1.call-done) | data formatting | bytes 4194304 | tf_op jit(solution)/shard_map/all_gather | solution.py:47
  49.4 0.5 broadcast.47
  49.9 45.2 %reduce.1 = bf16[8192,128]{1,0:T(8,128)(2,1)S(1)} reduce(bf16[8192,1,128]{2,1,0:T(2,128)(2,1)} %bitcast.91, bf16[]{:T(256)} %broadcast.47), dimensions={1}, to_apply=%bitcast.83.reduce_sub_computation | reduce | bytes 4194306
  95.1 2.1 reshape.85
  97.2 4.7 %all-to-all-start = ((bf16[4,2,131072]{2,1,0:T(2,128)(2,1)}), bf16[4,2,131072]{2,1,0:T(2,128)(2,1)S(1)}, u32[]{:S(2)}, u32[]{:S(2)}) async-start(bf16[4,2,131072]{2,1,0:T(2,128)(2,1)} %reshape.85), calls=%async_computation | async-start | bytes 4194304 | tf_op jit(solution)/shard_map/all_to_all | solution.py:51
  101.9 0.6 dynamic-slice
  103.2 0.7 dynamic-slice_convert_fusion
  103.9 1.5 multiply_reduce_fusion
  105.5 36.9 %all-reduce = f32[256]{0:T(256)S(1)} all-reduce(f32[256]{0:T(256)S(1)} %rsqrt_dynamic-update-slice_fusion), channel_id=2, replica_groups=mesh['prompt'=4,'tensor'=8] {'prompt'}, use_global_device_ids=true, to_apply=%add | all-reduce | flops 256 | bytes 2048
  142.5 8.3 %all-to-all-done = bf16[4,2,131072]{2,1,0:T(2,128)(2,1)S(1)} async-done(((bf16[4,2,131072]{2,1,0:T(2,128)(2,1)}), bf16[4,2,131072]{2,1,0:T(2,128)(2,1)S(1)}, u32[]{:S(2)}, u32[]{:S(2)}) %all-to-all-start) | async-done | bytes 2097184 | tf_op jit(solution)/shard_map/all_to_all | solution.py:51
  150.8 3.4 reshape.86
  154.1 2.5 copy.67
  156.6 2.7 copy.49
  159.3 1.9 fusion.18
  161.3 0.5 fusion.19
  161.8 3.6 fusion.4
  165.4 1.3 fusion.2
  166.7 1.6 pad_maximum_fusion
  168.4 48.5 %reduce-scatter.4.cloned.1.call-done = f32[1,64,2304]{2,1,0:T(8,128)} async-done(((f32[4,64,2304]{2,1,0:T(8,128)}), f32[1,64,2304]{2,1,0:T(8,128)}) %reduce-scatter.4.cloned.1.call-update) | async-done | bytes 589840 | tf_op jit(solution)/shard_map/reduce_scatter | solution.py:67
  217.0 1.1 convert_bitcast_fusion
  218.1 9.5 %all-gather.1 = bf16[512,256]{1,0:T(8,128)(2,1)S(1)} all-gather(bf16[64,256]{1,0:T(8,128)(2,1)S(1)} %slice.55), channel_id=3, replica_groups=mesh['prompt'=4,'tensor'=8] {'tensor'}, dimensions={0}, use_global_device_ids=true | all-gather | bytes 294912 | tf_op jit(solution)/shard_map/all_gather | solution.py:72
  227.7 0.2 fusion.31
  227.9 0.2 convolution_multiply_fusion
  228.1 0.7 copy-done.4
  228.8 0.8 fusion.85
  229.6 1.4 convolution_bitcast_fusion
  231.0 1.4 convolution_bitcast_fusion.1
  232.4 0.7 maximum_bitcast_fusion
  233.2 1.7 fusion.14
  235.0 29.7 %reduce-scatter.6.cloned.1.call-done = f32[2,20,128]{2,1,0:T(8,128)} async-done(((f32[2,20,1024]{2,1,0:T(8,128)}), f32[2,20,128]{2,1,0:T(8,128)}) %reduce-scatter.6.cloned.1.call-update) | async-done | bytes 20496 | tf_op jit(solution)/shard_map/reduce_scatter | solution.py:110
  264.6 0.7 convert_element_type.69
  265.4 13.9 %all-gather.3 = bf16[4,20,1280]{2,1,0:T(8,128)(2,1)S(1)} all-gather(bf16[1,20,1280]{2,1,0:T(8,128)(2,1)S(1)} %maximum_bitcast_fusion.1), channel_id=1, replica_groups=mesh['prompt'=4,'tensor'=8] {'prompt'}, dimensions={0}, use_global_device_ids=true | all-gather | bytes 256000 | tf_op jit(solution)/shard_map/all_gather | solution.py:113
  279.3 0.3 fusion.49
  279.6 1.3 fusion.51
  280.9 4.4 %fusion.6 = f32[80,2048]{1,0:T(8,128)} fusion(f32[80,2048]{1,0:T(8,128)S(1)} %fusion.49, f32[80,2048]{1,0:T(8,128)S(1)} %fusion.51, bf16[2048,1024]{1,0:T(8,128)(2,1)} %param.12, bf16[80,1280]{1,0:T(8,128)(2,1)S(1)} %reshape.77), kind=kOutput, calls=%fused_computation.7 | convolution fusion | flops 335872000 | bytes 6324224 | tf_op jit(solution)/shard_map/nc,dc->nd/dot_general | solution.py:18
  285.6 11.1 %all-gather.2 = s32[4,1,20]{2,1,0:T(1,128)S(1)} all-gather(s32[1,1,20]{2,1,0:T(1,128)S(1)} %bitcast.112), channel_id=1, replica_groups=mesh['prompt'=4,'tensor'=8] {'prompt'}, dimensions={0}, use_global_device_ids=true | all-gather | bytes 400 | tf_op jit(solution)/shard_map/all_gather | solution.py:45
  296.7 0.2 select_reduce_fusion.1
  297.0 0.2 convolution_multiply_fusion.1
  297.2 23.2 %reduce-scatter.8.cloned.1.call-done = f32[80,256]{1,0:T(8,128)} async-done(((f32[80,2048]{1,0:T(8,128)}), f32[80,256]{1,0:T(8,128)}) %reduce-scatter.8.cloned.1.call-update) | async-done | bytes 81936 | tf_op jit(solution)/shard_map/reduce_scatter | solution.py:117
  320.5 1.0 multiply_reduce_fusion.2
  321.5 12.3 %psum.14 = f32[80,1]{0,1:T(1,128)S(1)} all-reduce(f32[80,1]{0,1:T(1,128)S(1)} %bitcast.108), channel_id=1, replica_groups=mesh['prompt'=4,'tensor'=8] {'tensor'}, use_global_device_ids=true, to_apply=%region_9.10 | all-reduce | flops 80 | bytes 640 | tf_op jit(solution)/shard_map/psum | solution.py:13
  333.7 11.7 %psum.15 = f32[80,1]{0,1:T(1,128)S(1)} all-reduce(f32[80,1]{0,1:T(1,128)S(1)} %psum.14), channel_id=1, replica_groups=mesh['prompt'=4,'tensor'=8] {'prompt'}, use_global_device_ids=true, to_apply=%region_10.11 | all-reduce | flops 80 | bytes 640 | tf_op jit(solution)/shard_map/psum | solution.py:14
  345.4 1.6 multiply_convert_fusion.4
  347.1 51.1 %all-gather.9.cloned.1.call-done = bf16[80,8192]{1,0:T(8,128)(2,1)} async-done(((bf16[80,256]{1,0:T(8,128)(2,1)}), bf16[80,8192]{1,0:T(8,128)(2,1)}) %all-gather.9.cloned.1.call-update) | async-done | bytes 1310736 | tf_op jit(solution)/shard_map/all_gather | solution.py:133
  398.2 15.3 %convolution_negate_fusion = f32[80,2048]{1,0:T(8,128)S(1)} fusion(bf16[80,8192]{1,0:T(8,128)(2,1)} %all-gather.9.cloned.1.call-done, bf16[2048,8192]{1,0:T(8,128)(2,1)} %param.18), kind=kOutput, calls=%fused_computation.8 | convolution fusion | flops 2684518400 | bytes 35520512 | tf_op jit(solution)/shard_map/rd,vd->rv/dot_general | solution.py:18
  413.6 1.3 copy.63
  (53 shorter events, 1.3 us)
Async XLA Ops:
  6.5 152.8 %copy-start = (bf16[2048,128]{1,0:T(8,128)(2,1)S(1)}, bf16[2048,128]{1,0:T(8,128)(2,1)}, u32[]{:S(2)}) copy-start(bf16[2048,128]{1,0:T(8,128)(2,1)} %param.14) | copy-start | bytes 1572868
  6.5 33.4 %all-gather.7.cloned.1.call-start = ((), (), s32[]{:S(2)}) async-start(), calls=%async_computation.4 | async-start | bytes 2359296 | tf_op jit(solution)/shard_map/all_gather | solution.py:47
  97.2 4.7 %copy-start.8 = (u32[32]{0:T(128)S(1)}, u32[32]{0:T(128)}, u32[]{:S(2)}) copy-start(u32[32]{0:T(128)} %constant.38) | copy-start | bytes 388
  97.2 53.6 %all-to-all-start = ((bf16[4,2,131072]{2,1,0:T(2,128)(2,1)}), bf16[4,2,131072]{2,1,0:T(2,128)(2,1)S(1)}, u32[]{:S(2)}, u32[]{:S(2)}) async-start(bf16[4,2,131072]{2,1,0:T(2,128)(2,1)} %reshape.85), calls=%async_computation | async-start | bytes 4194304 | tf_op jit(solution)/shard_map/all_to_all | solution.py:51
  101.9 115.0 %reduce-scatter.4.cloned.1.call-start = ((), (), s32[]{:S(2)}) async-start(), calls=%async_computation.5 | async-start | bytes 2949120 | tf_op jit(solution)/shard_map/reduce_scatter | solution.py:67
  159.3 1.9 copy-start.1
  159.3 2.0 copy-start.2
  161.8 3.7 copy-start.7
  168.4 96.2 %reduce-scatter.6.cloned.1.call-start = ((), (), s32[]{:S(2)}) async-start(), calls=%async_computation.6 | async-start | bytes 221184 | tf_op jit(solution)/shard_map/reduce_scatter | solution.py:110
  168.4 61.2 %copy-start.6 = (s32[1,20]{1,0:T(1,128)S(1)}, s32[1,20]{1,0:T(1,128)}, u32[]{:S(2)}) copy-start(s32[1,20]{1,0:T(1,128)} %param.17) | copy-start | bytes 244
  227.9 3.1 copy-start.3
  228.1 0.7 copy-start.4
  233.2 87.3 %reduce-scatter.8.cloned.1.call-start = ((), (), s32[]{:S(2)}) async-start(), calls=%async_computation.7 | async-start | bytes 737280 | tf_op jit(solution)/shard_map/reduce_scatter | solution.py:117
  285.4 61.7 %copy-start.5 = (s32[2048]{0:T(1024)S(1)}, s32[2048]{0:T(1024)}, u32[]{:S(2)}) copy-start(s32[2048]{0:T(1024)} %param.19) | copy-start | bytes 24580
  285.4 112.8 %all-gather.9.cloned.1.call-start = ((), (), s32[]{:S(2)}) async-start(), calls=%async_computation.8 | async-start | bytes 1351680 | tf_op jit(solution)/shard_map/all_gather | solution.py:133
Sparse Core Ops, SparseCore 0:
  9.3 30.5 all-gather.6
  168.5 48.4 reduce-scatter.3
  233.3 31.2 reduce-scatter.5
  285.5 34.8 reduce-scatter.7
  347.2 50.9 all-gather.8
